TPU v7x, 512 devices: a whole 4x8x8 slice. The times are simulated.
512 devices in a mesh: au: 32 (over z, y_lo), ia: 16 (over x, y_hi, core).
Axes of the slice: x: 4, y: 8 (y_hi: 2, y_lo: 4; y = y_hi * 4 + y_lo), z: 8, core: 2. Of those that a mesh axis runs over, the one named last changes fastest.
Arguments:
- user_emb: bfloat16 [32, 2048, 256], P('au', 'ia'), may hold values from -6 to 6
- item_emb: bfloat16 [16, 1024, 256], P('ia', 'au'), may hold values from -6 to 6
- weight: bfloat16 [256, 256], replicated, may hold values from -0.375 to 0.375
- grad_user: bfloat16 [32, 2048, 256], P('au', 'ia'), may hold values from -6 to 6
- grad_item: bfloat16 [16, 1024, 256], P('ia', 'au'), may hold values from -6 to 6
- tile_values: bfloat16 [32, 2048, 128, 128], P('au', 'ia'), may hold values from 0 to 1
- tile_rows: int32 [32, 2048], P('au', 'ia'), may hold values from 0 to 15
- tile_cols: int32 [32, 2048], P('au', 'ia'), may hold values from 0 to 7
- tile_norm: int32 [32, 2048], P('au', 'ia'), may hold values from 32 to 128
- tile_count: int32 [32, 16], P('au', 'ia'), may hold values from 64 to 128, as said below
Outputs:
- grad_user_emb: bfloat16 [32, 2048, 256], P('au', 'ia')
- grad_item_emb: bfloat16 [16, 1024, 256], P('ia', 'au')
- grad_weight: float32 [256, 256], replicated
Inputs may be any that keep to these rules, and one draw needn't show every extreme that they name: `tile_rows`: slots of one block pair may name the same tile position; their terms add. Slots at and after tile_count[a, b] are unused; some block pair has exactly 128 live slots in every draw.
All inputs are finite; a program needn't handle non-finite values.
Results may differ from a plain program's by a relative error of at most 0.025.
Values may be sent and summed in bfloat16 or wider, within the bound.
No kernel may reach another device: no remote copies, remote signals or barrier semaphores. Data moves between devices by JAX's collectives and lax.ppermute only.
A program may use at most 64 MiB of HBM per device.

v0:
```python
import math
import jax
import jax.numpy as jnp
from jax import lax
from jax.sharding import PartitionSpec as P

slot_group = 8


def from_everyone(value, axis):
    copies = jnp.broadcast_to(value, (lax.axis_size(axis), *value.shape))
    return lax.all_to_all(copies, axis, split_axis=0, concat_axis=0, tiled=True)


def in_order(pieces, dim):
    pieces = jnp.moveaxis(pieces, 0, dim)
    shape = pieces.shape
    return pieces.reshape(*shape[:dim], shape[dim] * shape[dim + 1], *shape[dim + 2 :])


def collect(value, axis, dim):
    pieces = from_everyone(value, axis)
    return in_order(pieces, dim)


def in_blocks(value, dim, peers):
    shape = value.shape
    pieces = value.reshape(*shape[:dim], peers, shape[dim] // peers, *shape[dim + 1 :])
    return jnp.moveaxis(pieces, dim, 0)


def summed_on_arrival(value, axis, dim):
    pieces = in_blocks(value, dim, lax.axis_size(axis))
    arrived = lax.all_to_all(pieces, axis, split_axis=0, concat_axis=0, tiled=True)
    return arrived.astype(jnp.float32).sum(axis=0)


def split_tiles(block, edge):
    return block.reshape(-1, edge, block.shape[-1])


def fetch_items(grad_item, edge):
    cotangent = collect(grad_item, "au", 1)
    return (split_tiles(cotangent[0], edge), None)


def fetch_users(grad_user, edge):
    cotangent = collect(grad_user, "ia", 1)
    return (split_tiles(cotangent[0], edge), None)


def sweep(
    tile_block,
    row_ids,
    col_ids,
    norm_ids,
    live_count,
    item_source,
    user_source,
    user_shape,
    item_shape,
):
    turn_count = (live_count + slot_group - 1) // slot_group
    placeholder = jnp.zeros((1,), jnp.float32)

    def one_turn(turn_index, totals):
        user_total, item_total = totals
        first_slot = turn_index * slot_group
        values = lax.dynamic_slice_in_dim(tile_block, first_slot, slot_group, 0)
        row_pick = lax.dynamic_slice_in_dim(row_ids, first_slot, slot_group, 0)
        col_pick = lax.dynamic_slice_in_dim(col_ids, first_slot, slot_group, 0)
        norm_pick = lax.dynamic_slice_in_dim(norm_ids, first_slot, slot_group, 0)
        live_mask = first_slot + jnp.arange(slot_group, dtype=jnp.int32) < live_count
        inverse = jnp.where(live_mask, 1.0 / norm_pick.astype(jnp.float32), 0.0)[:, None, None]
        if item_source is not None:
            forward = jnp.einsum(
                "gic,gcd->gid", values, item_source[col_pick], preferred_element_type=jnp.float32
            )
            user_total = user_total.at[row_pick].add(forward * inverse)
        if user_source is not None:
            backward = jnp.einsum(
                "gic,gid->gcd", values, user_source[row_pick], preferred_element_type=jnp.float32
            )
            item_total = item_total.at[col_pick].add(backward * inverse)
        return (user_total, item_total)

    start = (
        jnp.zeros(user_shape, jnp.float32) if item_source is not None else placeholder,
        jnp.zeros(item_shape, jnp.float32) if user_source is not None else placeholder,
    )
    return lax.fori_loop(0, turn_count, one_turn, start)


def reduce_users(user_total, width):
    return summed_on_arrival(user_total.reshape(-1, width).astype(jnp.bfloat16), "ia", 0)


def reduce_items(item_total, width):
    return summed_on_arrival(item_total.reshape(-1, width).astype(jnp.bfloat16), "au", 0)


def block_product(embedded, total):
    return jnp.einsum(
        "rd,re->de", embedded.astype(jnp.float32), total, precision=lax.Precision.HIGHEST
    )


def per_device(
    user_emb,
    item_emb,
    weight,
    grad_user,
    grad_item,
    tile_values,
    tile_rows,
    tile_cols,
    tile_norm,
    tile_count,
):
    width = weight.shape[0]
    edge = tile_values.shape[2]
    user_shape = (user_emb.shape[1] * lax.axis_size("ia") // edge, edge, width)
    item_shape = (item_emb.shape[1] * lax.axis_size("au") // edge, edge, width)
    tile_block = tile_values[0]
    row_ids = tile_rows[0]
    col_ids = tile_cols[0]
    norm_ids = tile_norm[0]
    live_count = tile_count[0, 0]
    item_source, item_rows = fetch_items(grad_item, edge)
    user_total, unused = sweep(
        tile_block,
        row_ids,
        col_ids,
        norm_ids,
        live_count,
        item_source,
        None,
        user_shape,
        item_shape,
    )
    q_user = reduce_users(user_total, width)
    user_source, user_rows = fetch_users(grad_user, edge)
    unused, item_total = sweep(
        tile_block,
        row_ids,
        col_ids,
        norm_ids,
        live_count,
        None,
        user_source,
        user_shape,
        item_shape,
    )
    q_item = reduce_items(item_total, width)
    weight_part = block_product(user_emb[0], q_user) + block_product(item_emb[0], q_item)
    user_count = user_emb.shape[1] * lax.axis_size("ia") * lax.axis_size("au")
    item_count = item_emb.shape[1] * lax.axis_size("au") * lax.axis_size("ia")
    grad_weight = lax.psum(weight_part, ("au", "ia")) / math.sqrt(user_count + item_count)
    grad_user_emb = jnp.einsum(
        "re,de->rd", q_user.astype(jnp.bfloat16), weight, preferred_element_type=jnp.float32
    ).astype(jnp.bfloat16)
    grad_item_emb = jnp.einsum(
        "re,de->rd", q_item.astype(jnp.bfloat16), weight, preferred_element_type=jnp.float32
    ).astype(jnp.bfloat16)
    return (grad_user_emb[None], grad_item_emb[None], grad_weight)


def solution(mesh):
    return jax.shard_map(
        per_device,
        mesh=mesh,
        in_specs=(
            P("au", "ia", None),
            P("ia", "au", None),
            P(),
            P("au", "ia", None),
            P("ia", "au", None),
            P("au", "ia", None, None),
            P("au", "ia"),
            P("au", "ia"),
            P("au", "ia"),
            P("au", "ia"),
        ),
        out_specs=(P("au", "ia", None), P("ia", "au", None), P()),
        check_vma=False,
    )
```

profile of v0, /device:TPU:23, one launch (start us, length us, event | category | flops | bytes accessed | tf_op | source)
XLA Modules:
  0.0 567.4 jit_solution(4700820097756876434)
XLA Ops:
  7.2 2.0 broadcast_in_dim.43
  9.2 8.5 %all-to-all-start.2 = ((bf16[16,1,128,256]{3,2,1,0:T(8,128)(2,1)}), bf16[16,1,128,256]{3,2,1,0:T(8,128)(2,1)}, u32[]{:S(2)}, u32[]{:S(2)}) async-start(bf16[16,1,128,256]{3,2,1,0:T(8,128)(2,1)} %broadcast_in_dim.43), calls=%async_computation.2 | async-start | bytes 2097152 | tf_op jit(solution)/shard_map/all_to_all | solution.py:12
  18.4 6.4 %copy.16 = bf16[1,128,128,128]{2,3,1,0:T(8,128)(2,1)} copy(bf16[1,128,128,128]{3,2,1,0:T(8,128)(2,1)} %param.19) | data formatting | bytes 8388608 | tf_op args[5]
  24.8 21.8 %all-to-all-done.2 = bf16[16,1,128,256]{3,2,1,0:T(8,128)(2,1)} async-done(((bf16[16,1,128,256]{3,2,1,0:T(8,128)(2,1)}), bf16[16,1,128,256]{3,2,1,0:T(8,128)(2,1)}, u32[]{:S(2)}, u32[]{:S(2)}) %all-to-all-start.2) | async-done | bytes 1048608 | tf_op jit(solution)/shard_map/all_to_all | solution.py:12
  47.4 12.4 %all-to-all-start = ((bf16[32,1,32,256]{3,2,1,0:T(8,128)(2,1)}), bf16[32,1,32,256]{3,2,1,0:T(8,128)(2,1)S(1)}, u32[]{:S(2)}, u32[]{:S(2)}) async-start(bf16[32,1,32,256]{3,2,1,0:T(8,128)(2,1)} %broadcast_in_dim.40), calls=%async_computation | async-start | bytes 1048576 | tf_op jit(solution)/shard_map/all_to_all | solution.py:12
  59.9 68.0 %while.21 = (s32[]{:T(128)}, f32[8,128,256]{2,1,0:T(8,128)S(1)}, s32[]{:T(128)}, s32[128]{0:T(128)S(1)}, bf16[128,128,128]{1,2,0:T(8,128)(2,1)}, /*index=5*/s32[...) while((s32[]{:T(128)}, f32[8,128,256]{2,1,0:T(8,128)S(1)}, ...), condition=%wide.region_6.7_spmd, body=%wide.region_4.6_spmd.sunk | while | flops 67634272 | bytes 6033919 | solution.py:91
  60.8 1.8 gather_fusion.1
  63.8 1.3 scatter_fusion.1
  66.0 1.8 gather_fusion.1
  69.1 1.3 scatter_fusion.1
  71.2 1.8 gather_fusion.1
  73.1 1.2 convolution_multiply_fusion.5
  74.3 1.3 scatter_fusion.1
  76.5 1.8 gather_fusion.1
  78.3 1.2 convolution_multiply_fusion.5
  79.5 1.3 scatter_fusion.1
  81.7 1.8 gather_fusion.1
  84.8 1.3 scatter_fusion.1
  86.9 1.8 gather_fusion.1
  88.8 1.2 convolution_multiply_fusion.5
  90.0 1.3 scatter_fusion.1
  92.2 1.8 gather_fusion.1
  94.0 1.2 convolution_multiply_fusion.5
  95.2 1.3 scatter_fusion.1
  97.4 1.8 gather_fusion.1
  100.5 1.3 scatter_fusion.1
  102.6 1.8 gather_fusion.1
  104.4 1.2 convolution_multiply_fusion.5
  105.7 1.3 scatter_fusion.1
  107.8 1.8 gather_fusion.1
  110.9 1.3 scatter_fusion.1
  113.1 1.8 gather_fusion.1
  116.1 1.3 scatter_fusion.1
  118.3 1.8 gather_fusion.1
  120.1 1.2 convolution_multiply_fusion.5
  121.4 1.3 scatter_fusion.1
  123.5 1.8 gather_fusion.1
  126.6 1.3 scatter_fusion.1
  128.8 24.3 %all-to-all-start.3 = ((bf16[32,32,256]{2,1,0:T(8,128)(2,1)}), bf16[32,32,256]{2,1,0:T(8,128)(2,1)S(1)}, u32[]{:S(2)}, u32[]{:S(2)}) async-start(bf16[32,32,256]{2,1,0:T(8,128)(2,1)} %bitcast.11), calls=%async_computation.3 | async-start | bytes 1048576 | tf_op jit(solution)/shard_map/all_to_all | solution.py:34
  153.1 1.6 broadcast_in_dim.39
  154.7 77.1 %while.20 = (s32[]{:T(128)}, f32[16,128,256]{2,1,0:T(8,128)}, s32[]{:T(128)}, s32[128]{0:T(128)S(1)}, bf16[128,128,128]{2,1,0:T(8,128)(2,1)}, /*index=5*/s32[128...) while((s32[]{:T(128)}, f32[16,128,256]{2,1,0:T(8,128)}, ...), condition=%wide.region_2.3_spmd, body=%wide.region_0.2_spmd.sunk | while | flops 67634272 | bytes 6033919 | solution.py:91
  156.1 1.2 convolution_multiply_fusion.4
  157.3 3.3 scatter_fusion
  163.2 3.3 scatter_fusion
  167.9 1.2 convolution_multiply_fusion.4
  169.2 3.3 scatter_fusion
  173.9 1.2 convolution_multiply_fusion.4
  175.1 3.3 scatter_fusion
  179.8 1.2 convolution_multiply_fusion.4
  181.0 3.3 scatter_fusion
  187.0 3.3 scatter_fusion
  192.9 3.2 scatter_fusion
  197.6 1.2 convolution_multiply_fusion.4
  198.8 3.3 scatter_fusion
  204.7 3.3 scatter_fusion
  210.6 3.3 scatter_fusion
  216.6 3.3 scatter_fusion
  222.6 3.3 scatter_fusion
  227.2 1.2 convolution_multiply_fusion.4
  228.5 3.3 scatter_fusion
  231.8 2.7 convert_element_type.37
  234.5 23.4 %all-to-all-start.1 = ((bf16[16,128,256]{2,1,0:T(8,128)(2,1)}), bf16[16,128,256]{2,1,0:T(8,128)(2,1)S(1)}, u32[]{:S(2)}, u32[]{:S(2)}) async-start(bf16[16,128,256]{2,1,0:T(8,128)(2,1)} %convert_element_type.37), calls=%async_computation.1 | async-start | bytes 2097152 | tf_op jit(solution)/shard_map/all_to_all | solution.py:34
  258.3 27.8 %all-to-all-done.1 = bf16[16,128,256]{2,1,0:T(8,128)(2,1)S(1)} async-done(((bf16[16,128,256]{2,1,0:T(8,128)(2,1)}), bf16[16,128,256]{2,1,0:T(8,128)(2,1)S(1)}, u32[]{:S(2)}, u32[]{:S(2)}) %all-to-all-start.1) | async-done | bytes 1048608 | tf_op jit(solution)/shard_map/all_to_all | solution.py:34
  289.0 269.7 %all-reduce.2.cloned.1.call-done = f32[256,256]{0,1:T(8,128)} async-done(((f32[256,256]{0,1:T(8,128)}), f32[256,256]{0,1:T(8,128)}) %all-reduce.2.cloned.1.call-update) | async-done | bytes 262160 | tf_op jit(solution)/shard_map/psum | solution.py:158
  (134 shorter events, 52.7 us)
Async XLA Ops:
  7.2 280.2 %copy-start = (bf16[256,256]{1,0:T(8,128)(2,1)S(1)}, bf16[256,256]{1,0:T(8,128)(2,1)}, u32[]{:S(2)}) copy-start(bf16[256,256]{1,0:T(8,128)(2,1)} %param.16) | copy-start | bytes 393220
  9.2 37.4 %all-to-all-start.2 = ((bf16[16,1,128,256]{3,2,1,0:T(8,128)(2,1)}), bf16[16,1,128,256]{3,2,1,0:T(8,128)(2,1)}, u32[]{:S(2)}, u32[]{:S(2)}) async-start(bf16[16,1,128,256]{3,2,1,0:T(8,128)(2,1)} %broadcast_in_dim.43), calls=%async_computation.2 | async-start | bytes 2097152 | tf_op jit(solution)/shard_map/all_to_all | solution.py:12
  18.4 28.2 %copy-start.5 = (bf16[1,32,256]{2,1,0:T(8,128)(2,1)S(1)}, bf16[1,32,256]{2,1,0:T(8,128)(2,1)}, u32[]{:S(2)}) copy-start(bf16[1,32,256]{2,1,0:T(8,128)(2,1)} %param.18) | copy-start | bytes 49156
  24.7 35.2 %copy-start.2 = (s32[1,128]{1,0:T(1,128)S(1)}, s32[1,128]{1,0:T(1,128)}, u32[]{:S(2)}) copy-start(s32[1,128]{1,0:T(1,128)} %param.20) | copy-start | bytes 1540
  24.8 35.2 %copy-start.3 = (s32[1,128]{1,0:T(1,128)S(1)}, s32[1,128]{1,0:T(1,128)}, u32[]{:S(2)}) copy-start(s32[1,128]{1,0:T(1,128)} %param.21) | copy-start | bytes 1540
  24.8 35.2 %copy-start.4 = (s32[1,128]{1,0:T(1,128)S(1)}, s32[1,128]{1,0:T(1,128)}, u32[]{:S(2)}) copy-start(s32[1,128]{1,0:T(1,128)} %param.22) | copy-start | bytes 1540
  47.4 81.4 %all-to-all-start = ((bf16[32,1,32,256]{3,2,1,0:T(8,128)(2,1)}), bf16[32,1,32,256]{3,2,1,0:T(8,128)(2,1)S(1)}, u32[]{:S(2)}, u32[]{:S(2)}) async-start(bf16[32,1,32,256]{3,2,1,0:T(8,128)(2,1)} %broadcast_in_dim.40), calls=%async_computation | async-start | bytes 1048576 | tf_op jit(solution)/shard_map/all_to_all | solution.py:12
  128.8 105.7 %all-to-all-start.3 = ((bf16[32,32,256]{2,1,0:T(8,128)(2,1)}), bf16[32,32,256]{2,1,0:T(8,128)(2,1)S(1)}, u32[]{:S(2)}, u32[]{:S(2)}) async-start(bf16[32,32,256]{2,1,0:T(8,128)(2,1)} %bitcast.11), calls=%async_computation.3 | async-start | bytes 1048576 | tf_op jit(solution)/shard_map/all_to_all | solution.py:34
  234.5 23.5 %copy-start.6 = (bf16[1,32,256]{2,1,0:T(8,128)(2,1)S(1)}, bf16[1,32,256]{2,1,0:T(8,128)(2,1)}, u32[]{:S(2)}) copy-start(bf16[1,32,256]{2,1,0:T(8,128)(2,1)} %param.15) | copy-start | bytes 49156
  234.5 51.8 %copy-start.1 = (bf16[1,128,256]{2,1,0:T(8,128)(2,1)S(1)}, bf16[1,128,256]{2,1,0:T(8,128)(2,1)}, u32[]{:S(2)}) copy-start(bf16[1,128,256]{2,1,0:T(8,128)(2,1)} %param.14) | copy-start | bytes 196612
  234.5 51.7 %all-to-all-start.1 = ((bf16[16,128,256]{2,1,0:T(8,128)(2,1)}), bf16[16,128,256]{2,1,0:T(8,128)(2,1)S(1)}, u32[]{:S(2)}, u32[]{:S(2)}) async-start(bf16[16,128,256]{2,1,0:T(8,128)(2,1)} %convert_element_type.37), calls=%async_computation.1 | async-start | bytes 2097152 | tf_op jit(solution)/shard_map/all_to_all | solution.py:34
  257.9 300.8 %all-reduce.2.cloned.1.call-start = ((), (), s32[]{:S(2)}) async-start(), calls=%async_computation.4 | async-start | bytes 524288 | tf_op jit(solution)/shard_map/psum | solution.py:158
Sparse Core Ops, SparseCore 0:
  287.5 271.1 all-reduce.1
where the time goes:
time: 570 us; the launch traced here: 567 us
  waiting for transfers between devices  319 us (56%)
  other arithmetic  85.7 us (15%)
  starting transfers between devices  68.7 us (12%)
  local copies, waits for them, and re-layouts  42.9 us (8%)
  matrix products  35.1 us (6%)
  between operations  14.8 us (3%)
    psum x1, waiting for transfers between devices, per_device(): lax.psum(weight_part, ('au', 'ia')) / math.sqrt(user_count + item_count)  270 us
    all_to_all x2, starting transfers between devices, summed_on_arrival(): lax.all_to_all(pieces, axis, split_axis=0, concat_axis=0, tiled=True)  47.7 us
    scatter-add x13, other arithmetic, one_turn(): user_total = user_total.at[row_pick].add(forward * inverse)  42.8 us
    all_to_all x2, waiting for transfers between devices, summed_on_arrival(): lax.all_to_all(pieces, axis, split_axis=0, concat_axis=0, tiled=True)  27.8 us
    gather x13, local copies, waits for them, and re-layouts, one_turn(): user_source[row_pick]  23.5 us
    all_to_all x2, waiting for transfers between devices, from_everyone(): return lax.all_to_all(copies, axis, split_axis=0, concat_axis=0, tiled=True)  21.8 us
    all_to_all x2, starting transfers between devices, from_everyone(): return lax.all_to_all(copies, axis, split_axis=0, concat_axis=0, tiled=True)  20.9 us
    select_n x26, other arithmetic, one_turn(): jnp.where(live_mask, 1.0 / norm_pick.astype(jnp.float32), 0.0)  18.8 us
  transfers between devices with their start and end apart: 5, of which 3 were waited for; matrix products, arithmetic and copies ran while one was open for 28% of the time, Pallas kernels for 0%

commit v1 on v0

--- a/solution.py
+++ b/solution.py
@@ -155,7 +155,7 @@
     weight_part = block_product(user_emb[0], q_user) + block_product(item_emb[0], q_item)
     user_count = user_emb.shape[1] * lax.axis_size("ia") * lax.axis_size("au")
     item_count = item_emb.shape[1] * lax.axis_size("au") * lax.axis_size("ia")
-    grad_weight = lax.psum(weight_part, ("au", "ia")) / math.sqrt(user_count + item_count)
+    grad_weight = lax.psum(lax.psum(weight_part, "ia"), "au") / math.sqrt(user_count + item_count)
     grad_user_emb = jnp.einsum(
         "re,de->rd", q_user.astype(jnp.bfloat16), weight, preferred_element_type=jnp.float32
     ).astype(jnp.bfloat16)

time: 570 us -> 796 us (1.40)
  the two profiles are of different devices: /device:TPU:23 before, /device:TPU:2 now
where the time goes in v1:
time: 796 us; the launch traced here: 793 us
  waiting for transfers between devices  545 us (68%)
  other arithmetic  97.9 us (12%)
  local copies, waits for them, and re-layouts  47.7 us (6%)
  starting transfers between devices  46.7 us (6%)
  matrix products  40.1 us (5%)
  between operations  14.8 us (2%)
    psum x1, waiting for transfers between devices, per_device(): lax.psum(lax.psum(weight_part, 'ia'), 'au')  322 us
    psum x1, waiting for transfers between devices, per_device(): lax.psum(weight_part, 'ia')  180 us
    scatter-add x15, other arithmetic, one_turn(): user_total = user_total.at[row_pick].add(forward * inverse)  49.1 us
    gather x15, local copies, waits for them, and re-layouts, one_turn(): user_source[row_pick]  27.1 us
    all_to_all x2, starting transfers between devices, summed_on_arrival(): lax.all_to_all(pieces, axis, split_axis=0, concat_axis=0, tiled=True)  24.1 us
    all_to_all x2, waiting for transfers between devices, summed_on_arrival(): lax.all_to_all(pieces, axis, split_axis=0, concat_axis=0, tiled=True)  22.7 us
    all_to_all x2, starting transfers between devices, from_everyone(): return lax.all_to_all(copies, axis, split_axis=0, concat_axis=0, tiled=True)  22.5 us
    select_n x30, other arithmetic, one_turn(): jnp.where(live_mask, 1.0 / norm_pick.astype(jnp.float32), 0.0)  21.7 us
  transfers between devices with their start and end apart: 6, of which 4 were waited for; matrix products, arithmetic and copies ran while one was open for 23% of the time, Pallas kernels for 0%

profile of v1, /device:TPU:2, one launch (start us, length us, event | category | flops | bytes accessed | tf_op | source)
XLA Modules:
  0.0 793.0 jit_solution(13325222454458115610)
XLA Ops:
  7.2 2.0 broadcast_in_dim.43
  9.2 10.1 %all-to-all-start.2 = ((bf16[16,1,128,256]{3,2,1,0:T(8,128)(2,1)}), bf16[16,1,128,256]{3,2,1,0:T(8,128)(2,1)}, u32[]{:S(2)}, u32[]{:S(2)}) async-start(bf16[16,1,128,256]{3,2,1,0:T(8,128)(2,1)} %broadcast_in_dim.43), calls=%async_computation.2 | async-start | bytes 2097152 | tf_op jit(solution)/shard_map/all_to_all | solution.py:12
  20.0 6.4 copy.16
  26.3 20.5 %all-to-all-done.2 = bf16[16,1,128,256]{3,2,1,0:T(8,128)(2,1)} async-done(((bf16[16,1,128,256]{3,2,1,0:T(8,128)(2,1)}), bf16[16,1,128,256]{3,2,1,0:T(8,128)(2,1)}, u32[]{:S(2)}, u32[]{:S(2)}) %all-to-all-start.2) | async-done | bytes 1048608 | tf_op jit(solution)/shard_map/all_to_all | solution.py:12
  47.7 12.4 %all-to-all-start = ((bf16[32,1,32,256]{3,2,1,0:T(8,128)(2,1)}), bf16[32,1,32,256]{3,2,1,0:T(8,128)(2,1)S(1)}, u32[]{:S(2)}, u32[]{:S(2)}) async-start(bf16[32,1,32,256]{3,2,1,0:T(8,128)(2,1)} %broadcast_in_dim.40), calls=%async_computation | async-start | bytes 1048576 | tf_op jit(solution)/shard_map/all_to_all | solution.py:12
  60.3 78.4 %while.21 = (s32[]{:T(128)}, f32[8,128,256]{2,1,0:T(8,128)S(1)}, s32[]{:T(128)}, s32[128]{0:T(128)S(1)}, bf16[128,128,128]{1,2,0:T(8,128)(2,1)}, /*index=5*/s32[...) while((s32[]{:T(128)}, f32[8,128,256]{2,1,0:T(8,128)S(1)}, ...), condition=%wide.region_6.7_spmd, body=%wide.region_4.6_spmd.sunk | while | flops 67634272 | bytes 6033919 | solution.py:91
  61.1 1.8 gather_fusion.1
  64.2 1.3 scatter_fusion.1
  66.3 1.8 gather_fusion.1
  69.4 1.3 scatter_fusion.1
  71.6 1.8 gather_fusion.1
  74.6 1.3 scatter_fusion.1
  76.8 1.8 gather_fusion.1
  79.9 1.3 scatter_fusion.1
  82.0 1.8 gather_fusion.1
  85.1 1.3 scatter_fusion.1
  87.2 1.8 gather_fusion.1
  90.3 1.3 scatter_fusion.1
  92.5 1.8 gather_fusion.1
  95.5 1.3 scatter_fusion.1
  97.7 1.8 gather_fusion.1
  100.8 1.3 scatter_fusion.1
  102.9 1.8 gather_fusion.1
  104.7 1.2 convolution_multiply_fusion.5
  106.0 1.3 scatter_fusion.1
  108.2 1.8 gather_fusion.1
  110.0 1.2 convolution_multiply_fusion.5
  111.2 1.3 scatter_fusion.1
  113.4 1.8 gather_fusion.1
  116.4 1.3 scatter_fusion.1
  118.6 1.8 gather_fusion.1
  121.7 1.3 scatter_fusion.1
  123.8 1.8 gather_fusion.1
  126.9 1.3 scatter_fusion.1
  129.1 1.8 gather_fusion.1
  132.1 1.3 scatter_fusion.1
  134.3 1.8 gather_fusion.1
  136.1 1.2 convolution_multiply_fusion.5
  137.3 1.3 scatter_fusion.1
  139.5 10.5 %all-to-all-start.3 = ((bf16[32,32,256]{2,1,0:T(8,128)(2,1)}), bf16[32,32,256]{2,1,0:T(8,128)(2,1)S(1)}, u32[]{:S(2)}, u32[]{:S(2)}) async-start(bf16[32,32,256]{2,1,0:T(8,128)(2,1)} %bitcast.11), calls=%async_computation.3 | async-start | bytes 1048576 | tf_op jit(solution)/shard_map/all_to_all | solution.py:34
  150.1 1.6 broadcast_in_dim.39
  151.6 88.7 %while.20 = (s32[]{:T(128)}, f32[16,128,256]{2,1,0:T(8,128)}, s32[]{:T(128)}, s32[128]{0:T(128)S(1)}, bf16[128,128,128]{2,1,0:T(8,128)(2,1)}, /*index=5*/s32[128...) while((s32[]{:T(128)}, f32[16,128,256]{2,1,0:T(8,128)}, ...), condition=%wide.region_2.3_spmd, body=%wide.region_0.2_spmd.sunk | while | flops 67634272 | bytes 6033919 | solution.py:91
  154.3 3.2 scatter_fusion
  158.9 1.2 convolution_multiply_fusion.4
  160.2 3.2 scatter_fusion
  166.0 3.3 scatter_fusion
  172.0 3.3 scatter_fusion
  176.6 1.2 convolution_multiply_fusion.4
  177.9 3.3 scatter_fusion
  183.8 3.3 scatter_fusion
  189.7 3.3 scatter_fusion
  195.6 3.3 scatter_fusion
  201.6 3.2 scatter_fusion
  207.5 3.3 scatter_fusion
  213.4 3.3 scatter_fusion
  219.3 3.4 scatter_fusion
  225.3 3.2 scatter_fusion
  231.1 3.4 scatter_fusion
  237.1 3.2 scatter_fusion
  240.4 2.7 convert_element_type.37
  243.1 13.6 %all-to-all-start.1 = ((bf16[16,128,256]{2,1,0:T(8,128)(2,1)}), bf16[16,128,256]{2,1,0:T(8,128)(2,1)S(1)}, u32[]{:S(2)}, u32[]{:S(2)}) async-start(bf16[16,128,256]{2,1,0:T(8,128)(2,1)} %convert_element_type.37), calls=%async_computation.1 | async-start | bytes 2097152 | tf_op jit(solution)/shard_map/all_to_all | solution.py:34
  257.1 22.7 %all-to-all-done.1 = bf16[16,128,256]{2,1,0:T(8,128)(2,1)S(1)} async-done(((bf16[16,128,256]{2,1,0:T(8,128)(2,1)}), bf16[16,128,256]{2,1,0:T(8,128)(2,1)S(1)}, u32[]{:S(2)}, u32[]{:S(2)}) %all-to-all-start.1) | async-done | bytes 1048608 | tf_op jit(solution)/shard_map/all_to_all | solution.py:34
  281.0 179.6 %all-reduce.3.cloned.1.call-done = f32[256,256]{0,1:T(8,128)} async-done(((f32[256,256]{0,1:T(8,128)}), f32[256,256]{0,1:T(8,128)}) %all-reduce.3.cloned.1.call-update) | async-done | bytes 262160 | tf_op jit(solution)/shard_map/psum | solution.py:158
  462.3 322.0 %all-reduce.5.cloned.1.call-done = f32[256,256]{0,1:T(8,128)} async-done(((f32[256,256]{0,1:T(8,128)}), f32[256,256]{0,1:T(8,128)}) %all-reduce.5.cloned.1.call-update) | async-done | bytes 262160 | tf_op jit(solution)/shard_map/psum | solution.py:158
  (161 shorter events, 70.8 us)
Async XLA Ops:
  7.2 453.5 %copy-start = (bf16[256,256]{1,0:T(8,128)(2,1)S(1)}, bf16[256,256]{1,0:T(8,128)(2,1)}, u32[]{:S(2)}) copy-start(bf16[256,256]{1,0:T(8,128)(2,1)} %param.16) | copy-start | bytes 393220
  9.2 37.7 %all-to-all-start.2 = ((bf16[16,1,128,256]{3,2,1,0:T(8,128)(2,1)}), bf16[16,1,128,256]{3,2,1,0:T(8,128)(2,1)}, u32[]{:S(2)}, u32[]{:S(2)}) async-start(bf16[16,1,128,256]{3,2,1,0:T(8,128)(2,1)} %broadcast_in_dim.43), calls=%async_computation.2 | async-start | bytes 2097152 | tf_op jit(solution)/shard_map/all_to_all | solution.py:12
  19.9 26.9 %copy-start.5 = (bf16[1,32,256]{2,1,0:T(8,128)(2,1)S(1)}, bf16[1,32,256]{2,1,0:T(8,128)(2,1)}, u32[]{:S(2)}) copy-start(bf16[1,32,256]{2,1,0:T(8,128)(2,1)} %param.18) | copy-start | bytes 49156
  26.3 33.9 %copy-start.2 = (s32[1,128]{1,0:T(1,128)S(1)}, s32[1,128]{1,0:T(1,128)}, u32[]{:S(2)}) copy-start(s32[1,128]{1,0:T(1,128)} %param.20) | copy-start | bytes 1540
  26.3 33.9 %copy-start.3 = (s32[1,128]{1,0:T(1,128)S(1)}, s32[1,128]{1,0:T(1,128)}, u32[]{:S(2)}) copy-start(s32[1,128]{1,0:T(1,128)} %param.21) | copy-start | bytes 1540
  26.3 34.0 %copy-start.4 = (s32[1,128]{1,0:T(1,128)S(1)}, s32[1,128]{1,0:T(1,128)}, u32[]{:S(2)}) copy-start(s32[1,128]{1,0:T(1,128)} %param.22) | copy-start | bytes 1540
  47.7 91.8 %all-to-all-start = ((bf16[32,1,32,256]{3,2,1,0:T(8,128)(2,1)}), bf16[32,1,32,256]{3,2,1,0:T(8,128)(2,1)S(1)}, u32[]{:S(2)}, u32[]{:S(2)}) async-start(bf16[32,1,32,256]{3,2,1,0:T(8,128)(2,1)} %broadcast_in_dim.40), calls=%async_computation | async-start | bytes 1048576 | tf_op jit(solution)/shard_map/all_to_all | solution.py:12
  139.5 103.5 %all-to-all-start.3 = ((bf16[32,32,256]{2,1,0:T(8,128)(2,1)}), bf16[32,32,256]{2,1,0:T(8,128)(2,1)S(1)}, u32[]{:S(2)}, u32[]{:S(2)}) async-start(bf16[32,32,256]{2,1,0:T(8,128)(2,1)} %bitcast.11), calls=%async_computation.3 | async-start | bytes 1048576 | tf_op jit(solution)/shard_map/all_to_all | solution.py:34
  243.1 13.7 %copy-start.6 = (bf16[1,32,256]{2,1,0:T(8,128)(2,1)S(1)}, bf16[1,32,256]{2,1,0:T(8,128)(2,1)}, u32[]{:S(2)}) copy-start(bf16[1,32,256]{2,1,0:T(8,128)(2,1)} %param.15) | copy-start | bytes 49156
  243.1 36.8 %copy-start.1 = (bf16[1,128,256]{2,1,0:T(8,128)(2,1)S(1)}, bf16[1,128,256]{2,1,0:T(8,128)(2,1)}, u32[]{:S(2)}) copy-start(bf16[1,128,256]{2,1,0:T(8,128)(2,1)} %param.14) | copy-start | bytes 196612
  243.1 36.7 %all-to-all-start.1 = ((bf16[16,128,256]{2,1,0:T(8,128)(2,1)}), bf16[16,128,256]{2,1,0:T(8,128)(2,1)S(1)}, u32[]{:S(2)}, u32[]{:S(2)}) async-start(bf16[16,128,256]{2,1,0:T(8,128)(2,1)} %convert_element_type.37), calls=%async_computation.1 | async-start | bytes 2097152 | tf_op jit(solution)/shard_map/all_to_all | solution.py:34
  256.6 204.0 %all-reduce.3.cloned.1.call-start = ((), (), s32[]{:S(2)}) async-start(), calls=%async_computation.4 | async-start | bytes 524288 | tf_op jit(solution)/shard_map/psum | solution.py:158
  280.9 503.4 %all-reduce.5.cloned.1.call-start = ((), (), s32[]{:S(2)}) async-start(), calls=%async_computation.5 | async-start | bytes 524288 | tf_op jit(solution)/shard_map/psum | solution.py:158
Sparse Core Ops, SparseCore 0:
  281.1 179.5 all-reduce.2
  463.5 320.7 all-reduce.4
